TPU v7x, 256 devices: a whole 4x4x8 slice. The times are simulated.
256 devices in a mesh: dp: 4 (over y), mp: 64 (over x, z, core).
Axes of the slice: x: 4, y: 4, z: 8, core: 2. Of those that a mesh axis runs over, the one named last changes fastest.
Arguments:
- inputs: bfloat16 [8, 256, 6144], P('dp', None, 'mp'), may hold values from -6 to 6
- cotangent: bfloat16 [8, 256, 6144], P('dp', None, 'mp'), may hold values from -6 to 6
- w_up: bfloat16 [6144, 24576], P('dp', 'mp'), may hold values from -0.078125 to 0.078125
- w_down: bfloat16 [24576, 6144], P('mp', 'dp'), may hold values from -0.0390625 to 0.0390625
- thresholds: float32 [2], replicated, may hold values from 23592.96 to 58982.4
Outputs:
- grad_up: float32 [6144, 24576], P('dp', 'mp')
- grad_down: float32 [24576, 6144], P('mp', 'dp')
- norms: float32 [8, 2], P('dp')
All inputs are finite; a program needn't handle non-finite values.
Results may differ from a plain program's by a relative error of at most 0.0085.
Values may be sent and summed in bfloat16 or wider, within the bound.
A program may use at most 128 MiB of HBM per device.

v0:
```python
import jax
import jax.numpy as jnp
from jax import lax
from jax.sharding import PartitionSpec as P

inv_root_two = 0.7071067811865476
inv_root_two_pi = 0.3989422804014327


def sent_to_all(shard, axis):
    copies = jnp.broadcast_to(shard, (lax.axis_size(axis), *shard.shape))
    return lax.all_to_all(copies, axis, split_axis=0, concat_axis=0, tiled=True)


def taken_together(shard, axis):
    return sent_to_all(shard, axis).sum(axis=0)


def packed_total(arrays, axis):
    line, at, outs = (jnp.concatenate([a.reshape(-1) for a in arrays]), 0, [])
    running = taken_together(line, axis)
    for a in arrays:
        outs.append(running[at : at + a.size].reshape(a.shape))
        at += a.size
    return tuple(outs)


def split_up(shard, dim, count):
    shape = shard.shape
    pieces = shard.reshape(*shape[:dim], count, shape[dim] // count, *shape[dim + 1 :])
    return jnp.moveaxis(pieces, dim, 0)


def sum_at_owner(shard, axis, dim):
    pieces = split_up(shard, dim, lax.axis_size(axis))
    arrived = lax.all_to_all(pieces, axis, split_axis=0, concat_axis=0, tiled=True)
    return arrived.astype(jnp.float32).sum(axis=0)


def normal_cdf(value):
    return 0.5 * (1.0 + lax.erf(value * inv_root_two))


def gram_of(array, images, patches):
    cube = array.reshape(images, patches, -1)
    return jnp.einsum("btd,bsd->bts", cube, cube, preferred_element_type=jnp.float32)


def on_device(inputs, cotangent, w_up, w_down, thresholds):
    images, patches, local_feats = inputs.shape
    count_rows = images * patches
    x_whole = lax.all_gather(inputs, "mp", axis=2, tiled=True).reshape(count_rows, -1)
    hidden_local = w_up.shape[1]
    columns = x_whole
    pre = jnp.dot(
        columns, lax.all_gather(w_up, "dp", axis=0, tiled=True), preferred_element_type=jnp.float32
    )
    act = (pre * normal_cdf(pre)).astype(jnp.bfloat16)
    dy_whole = lax.all_gather(cotangent, "mp", axis=2, tiled=True).reshape(count_rows, -1)
    columns = dy_whole
    dact = lax.dot_general(
        columns,
        lax.all_gather(w_down, "dp", axis=1, tiled=True),
        (((1,), (1,)), ((), ())),
        preferred_element_type=jnp.float32,
    )
    slope = normal_cdf(pre) + pre * jnp.exp(-0.5 * pre * pre) * inv_root_two_pi
    dpre = (dact * slope).astype(jnp.bfloat16)
    gram_dpre = gram_of(dpre, images, patches)
    gram_act = gram_of(act, images, patches)
    part_up = jnp.sum(gram_of(x_whole, images, patches) * gram_dpre, axis=(1, 2))
    part_down = jnp.sum(gram_act * gram_of(dy_whole, images, patches), axis=(1, 2))
    sq_up, sq_down = packed_total((part_up, part_down), "mp")
    norms = jnp.stack([jnp.sqrt(sq_up), jnp.sqrt(sq_down)], axis=1)
    factor = jnp.minimum(1.0, thresholds[None, :] / (norms + 1e-06))
    dpre_clip = (
        (
            factor[:, 0][:, None, None]
            * dpre.reshape(images, patches, hidden_local).astype(jnp.float32)
        )
        .astype(jnp.bfloat16)
        .reshape(count_rows, hidden_local)
    )
    cot_clip = (
        (factor[:, 1][:, None, None] * dy_whole.reshape(images, patches, -1).astype(jnp.float32))
        .astype(jnp.bfloat16)
        .reshape(count_rows, -1)
    )
    columns = x_whole
    grad_up = lax.psum_scatter(
        lax.dot_general(
            columns, dpre_clip, (((0,), (0,)), ((), ())), preferred_element_type=jnp.float32
        ).astype(jnp.bfloat16),
        "dp",
        scatter_dimension=0,
        tiled=True,
    ).astype(jnp.float32)
    down_full = lax.dot_general(
        act, cot_clip, (((0,), (0,)), ((), ())), preferred_element_type=jnp.float32
    )
    grad_down = sum_at_owner(down_full.astype(jnp.bfloat16), "dp", 1)
    return (grad_up, grad_down, norms)


def solution(mesh):
    in_specs = (P("dp", None, "mp"), P("dp", None, "mp"), P("dp", "mp"), P("mp", "dp"), P())
    out_specs = (P("dp", "mp"), P("mp", "dp"), P("dp", None))
    return jax.shard_map(
        on_device, mesh=mesh, in_specs=in_specs, out_specs=out_specs, check_vma=False
    )
```

profile of v0, /device:TPU:1, one launch (start us, length us, event | category | flops | bytes accessed | tf_op | source)
XLA Modules:
  0.0 445.1 jit_solution(11769768210793305239)
XLA Ops:
  7.2 0.0 all-gather.5.cloned.1.call-start
  7.2 0.7 all-gather.5.cloned.1.call-update
  7.9 0.0 all-gather.7.cloned.1.call-start
  7.9 0.7 all-gather.7.cloned.1.call-update
  8.6 0.0 all-gather.11.cloned.1.call-start
  8.7 0.7 all-gather.11.cloned.1.call-update
  9.4 0.0 all-gather.9.cloned.1.call-start
  9.4 0.5 all-gather.9.cloned.1.call-update
  10.0 85.6 %all-gather.5.cloned.1.call-done = bf16[2,256,6144]{1,2,0:T(8,128)(2,1)} async-done(((bf16[2,256,96]{1,2,0:T(8,128)(2,1)}), bf16[2,256,6144]{1,2,0:T(8,128)(2,1)}) %all-gather.5.cloned.1.call-update) | async-done | bytes 6291472 | tf_op jit(solution)/shard_map/all_gather | solution.py:52
  95.5 8.7 %copy.32 = bf16[2,256,6144]{2,1,0:T(8,128)(2,1)} copy(bf16[2,256,6144]{1,2,0:T(8,128)(2,1)} %all-gather.5.cloned.1.call-done) | data formatting | bytes 12582912 | tf_op jit(solution)/shard_map/all_gather | solution.py:52
  104.2 71.4 %all-gather.7.cloned.1.call-done = bf16[2,256,6144]{1,2,0:T(8,128)(2,1)} async-done(((bf16[2,256,96]{1,2,0:T(8,128)(2,1)}), bf16[2,256,6144]{1,2,0:T(8,128)(2,1)}) %all-gather.7.cloned.1.call-update) | async-done | bytes 6291472 | tf_op jit(solution)/shard_map/all_gather | solution.py:59
  175.6 8.7 %copy.31 = bf16[2,256,6144]{2,1,0:T(8,128)(2,1)} copy(bf16[2,256,6144]{1,2,0:T(8,128)(2,1)} %all-gather.7.cloned.1.call-done) | data formatting | bytes 12582912 | tf_op jit(solution)/shard_map/all_gather | solution.py:59
  184.3 44.5 %all-gather.11.cloned.1.call-done = bf16[6144,384]{1,0:T(8,128)(2,1)} async-done(((bf16[1536,384]{1,0:T(8,128)(2,1)}), bf16[6144,384]{1,0:T(8,128)(2,1)}) %all-gather.11.cloned.1.call-update) | async-done | bytes 4718608 | tf_op jit(solution)/shard_map/all_gather | solution.py:56
  228.8 7.0 %multiply_convert_fusion.2 = (bf16[512,384]{1,0:T(8,128)(2,1)S(1)}, f32[512,384]{1,0:T(8,128)S(1)}) fusion(bf16[512,6144]{1,0:T(8,128)(2,1)} %bitcast.47, bf16[6144,384]{1,0:T(8,128)(2,1)} %all-gather.11.cloned.1.call-done), kind=kOutput, calls=%fused_computation.18 | convolution fusion | flops 2416902144 | bytes 12189696 | tf_op jit(solution)/shard_map/dot_general | solution.py:55
  235.7 50.3 %all-gather.9.cloned.1.call-done = bf16[384,6144]{1,0:T(8,128)(2,1)} async-done(((bf16[384,1536]{1,0:T(8,128)(2,1)}), bf16[384,6144]{1,0:T(8,128)(2,1)}) %all-gather.9.cloned.1.call-update) | async-done | bytes 4718608 | tf_op jit(solution)/shard_map/all_gather | solution.py:63
  286.0 7.7 %fusion.1 = bf16[512,384]{1,0:T(8,128)(2,1)S(1)} fusion(bf16[512,6144]{1,0:T(8,128)(2,1)} %bitcast.46, bf16[384,6144]{1,0:T(8,128)(2,1)} %all-gather.9.cloned.1.call-done, f32[512,384]{1,0:T(8,128)S(1)} %get-tuple-element.25), kind=kOutput, calls=%fused_computation.7 | convolution fusion | flops 2417885184 | bytes 12189696 | tf_op jit(solution)/shard_map/dot_general | solution.py:61
  293.7 0.3 fusion.9
  294.0 0.0 slice-start
  294.0 0.3 fusion.10
  294.4 0.0 slice-start.1
  294.4 7.4 %fusion.2 = f32[2]{0:T(128)S(1)} fusion(f32[2,256,256]{2,1,0:T(8,128)S(1)} %fusion.9, bf16[2,256,6144]{1,2,0:T(8,128)(2,1)} %all-gather.5.cloned.1.call-done), kind=kOutput, calls=%fused_computation.11 | convolution fusion | flops 1610874880 | bytes 6815752 | tf_op jit(solution)/shard_map/btd,bsd->bts/dot_general | solution.py:46
  301.8 0.0 slice-done
  301.8 0.0 slice-done.1
  301.8 0.0 copy-start
  301.8 2.7 fusion.3
  304.5 0.1 pad_maximum_fusion.1
  304.6 0.6 broadcast_in_dim.4
  305.2 10.8 %all-to-all-start = ((f32[64,1,4]{2,1,0:T(1,128)}), f32[64,1,4]{2,1,0:T(1,128)S(1)}, u32[]{:S(2)}, u32[]{:S(2)}) async-start(f32[64,1,4]{2,1,0:T(1,128)} %broadcast_in_dim.4), calls=%async_computation | async-start | bytes 65536 | tf_op jit(solution)/shard_map/all_to_all | solution.py:12
  316.1 0.2 reduce-scatter.2.cloned.1.call-start
  316.3 0.2 copy.34
  316.5 8.8 %all-to-all-done = f32[64,1,4]{2,1,0:T(1,128)S(1)} async-done(((f32[64,1,4]{2,1,0:T(1,128)}), f32[64,1,4]{2,1,0:T(1,128)S(1)}, u32[]{:S(2)}, u32[]{:S(2)}) %all-to-all-start) | async-done | bytes 1056 | tf_op jit(solution)/shard_map/all_to_all | solution.py:12
  325.3 0.1 reduce_sum.38
  325.4 0.1 sqrt_bitcast_fusion.1
  325.5 0.0 copy-done
  325.5 0.1 pad_maximum_fusion
  325.5 8.6 %fusion = bf16[6144,384]{0,1:T(8,128)(2,1)} fusion(bf16[2,256,6144]{1,2,0:T(8,128)(2,1)} %all-gather.5.cloned.1.call-done, bf16[2,256,384]{1,2,0:T(8,128)(2,1)S(1)} %copy.34, f32[2]{0:T(128)S(1)} %get-tuple-element.21), kind=kOutput, calls=%fused_computation.4 | convolution fusion | flops 2418868224 | bytes 11403272 | tf_op jit(solution)/shard_map/dot_general | solution.py:91
  334.2 0.0 reduce-scatter.2.cloned.1.call-update
  334.2 7.5 %multiply_convert_fusion = bf16[2,256,6144]{1,2,0:T(8,128)(2,1)} fusion(bf16[2,256,6144]{1,2,0:T(8,128)(2,1)} %all-gather.7.cloned.1.call-done, f32[2]{0:T(128)S(1)} %get-tuple-element.20), kind=kLoop, calls=%fused_computation | loop fusion | flops 9437184 | bytes 12582920 | tf_op jit(solution)/shard_map/convert_element_type | solution.py:86
  341.7 8.7 %copy.35 = bf16[2,256,6144]{2,1,0:T(8,128)(2,1)} copy(bf16[2,256,6144]{1,2,0:T(8,128)(2,1)} %multiply_convert_fusion) | data formatting | bytes 12582912 | tf_op jit(solution)/shard_map/convert_element_type | solution.py:86
  350.4 5.4 %convolution_convert_fusion = bf16[384,6144]{1,0:T(8,128)(2,1)S(1)} fusion(bf16[512,384]{1,0:T(8,128)(2,1)S(1)} %get-tuple-element.24, bf16[512,6144]{1,0:T(8,128)(2,1)} %bitcast.43), kind=kOutput, calls=%fused_computation.3 | convolution fusion | flops 2418278400 | bytes 11403264 | tf_op jit(solution)/shard_map/dot_general | solution.py:98
  355.8 2.6 copy.44
  358.4 4.9 %all-to-all-start.1 = ((bf16[4,384,1536]{2,1,0:T(8,128)(2,1)}), bf16[4,384,1536]{2,1,0:T(8,128)(2,1)}, u32[]{:S(2)}, u32[]{:S(2)}) async-start(bf16[4,384,1536]{2,1,0:T(8,128)(2,1)} %bitcast.44), calls=%async_computation.2 | async-start | bytes 9437184 | tf_op jit(solution)/shard_map/all_to_all | solution.py:36
  363.3 0.6 copy.38
  364.0 67.2 %all-to-all-done.1 = bf16[4,384,1536]{2,1,0:T(8,128)(2,1)} async-done(((bf16[4,384,1536]{2,1,0:T(8,128)(2,1)}), bf16[4,384,1536]{2,1,0:T(8,128)(2,1)}, u32[]{:S(2)}, u32[]{:S(2)}) %all-to-all-start.1) | async-done | bytes 4718624 | tf_op jit(solution)/shard_map/all_to_all | solution.py:36
  431.2 4.7 %convert_reduce_fusion = f32[384,1536]{1,0:T(8,128)} fusion(bf16[4,384,1536]{2,1,0:T(8,128)(2,1)} %all-to-all-done.1), kind=kLoop, calls=%fused_computation.2 | loop fusion | flops 4128768 | bytes 7077888 | tf_op jit(solution)/shard_map/reduce_sum | solution.py:37
  435.9 0.0 reduce-scatter.2.cloned.1.call-done
  435.9 2.7 copy.37
  (2 shorter events, 0.0 us)
Async XLA Ops:
  7.2 88.4 %all-gather.5.cloned.1.call-start = ((), (), s32[]{:S(2)}) async-start(), calls=%async_computation.3 | async-start | bytes 6389760 | tf_op jit(solution)/shard_map/all_gather | solution.py:52
  7.9 167.7 %all-gather.7.cloned.1.call-start = ((), (), s32[]{:S(2)}) async-start(), calls=%async_computation.4 | async-start | bytes 6389760 | tf_op jit(solution)/shard_map/all_gather | solution.py:59
  8.6 220.1 %all-gather.11.cloned.1.call-start = ((), (), s32[]{:S(2)}) async-start(), calls=%async_computation.6 | async-start | bytes 5898240 | tf_op jit(solution)/shard_map/all_gather | solution.py:56
  9.4 276.6 %all-gather.9.cloned.1.call-start = ((), (), s32[]{:S(2)}) async-start(), calls=%async_computation.5 | async-start | bytes 5898240 | tf_op jit(solution)/shard_map/all_gather | solution.py:63
  294.0 7.8 %slice-start = ((s8[6291456]{0:T(1024)(128)(4,1)}), s8[4194304]{0:T(1024)(128)(4,1)S(1)}, s32[]{:S(2)}) async-start(s8[6291456]{0:T(1024)(128)(4,1)} %bitcast.41), calls=%async_computation.8 | async-start | bytes 8388608
  294.4 7.4 %slice-start.1 = ((s8[6291456]{0:T(1024)(128)(4,1)}), s8[2097152]{0:T(1024)(128)(4,1)S(1)}, s32[]{:S(2)}) async-start(s8[6291456]{0:T(1024)(128)(4,1)} %bitcast.41), calls=%async_computation.9 | async-start | bytes 4194304
  301.8 23.7 %copy-start = (f32[2]{0:T(128)S(1)}, f32[2]{0:T(128)}, u32[]{:S(2)}) copy-start(f32[2]{0:T(128)} %param.9) | copy-start | bytes 28
  305.2 20.1 %all-to-all-start = ((f32[64,1,4]{2,1,0:T(1,128)}), f32[64,1,4]{2,1,0:T(1,128)S(1)}, u32[]{:S(2)}, u32[]{:S(2)}) async-start(f32[64,1,4]{2,1,0:T(1,128)} %broadcast_in_dim.4), calls=%async_computation | async-start | bytes 65536 | tf_op jit(solution)/shard_map/all_to_all | solution.py:12
  316.1 119.8 %reduce-scatter.2.cloned.1.call-start = ((), (), s32[]{:S(2)}) async-start(), calls=%async_computation.7 | async-start | bytes 5898240 | tf_op jit(solution)/shard_map/reduce_scatter | solution.py:90
  358.4 72.8 %all-to-all-start.1 = ((bf16[4,384,1536]{2,1,0:T(8,128)(2,1)}), bf16[4,384,1536]{2,1,0:T(8,128)(2,1)}, u32[]{:S(2)}, u32[]{:S(2)}) async-start(bf16[4,384,1536]{2,1,0:T(8,128)(2,1)} %bitcast.44), calls=%async_computation.2 | async-start | bytes 9437184 | tf_op jit(solution)/shard_map/all_to_all | solution.py:36
Sparse Core Ops, SparseCore 0:
  10.8 84.6 all-gather.4
  98.3 77.2 all-gather.6
  177.4 51.2 all-gather.10
  230.4 55.5 all-gather.8
  334.3 59.8 reduce-scatter.1
where the time goes:
time: 446 us; the launch traced here: 445 us
  waiting for transfers between devices  330 us (74%)
  matrix products  39.5 us (9%)
  local copies, waits for them, and re-layouts  32.9 us (7%)
  starting transfers between devices  16.1 us (4%)
  between operations  13.9 us (3%)
  other arithmetic  12.4 us (3%)
    all_gather x1, waiting for transfers between devices, on_device(): lax.all_gather(inputs, 'mp', axis=2, tiled=True).reshape(count_rows, -1)  85.6 us
    all_gather x1, waiting for transfers between devices, on_device(): lax.all_gather(cotangent, 'mp', axis=2, tiled=True).reshape(count_rows, -1)  71.4 us
    all_to_all x1, waiting for transfers between devices, sum_at_owner(): lax.all_to_all(pieces, axis, split_axis=0, concat_axis=0, tiled=True)  67.2 us
    all_gather x1, waiting for transfers between devices, on_device(): lax.all_gather(w_down, 'dp', axis=1, tiled=True)  50.3 us
    all_gather x1, waiting for transfers between devices, on_device(): lax.all_gather(w_up, 'dp', axis=0, tiled=True)  44.5 us
    all_to_all x1, starting transfers between devices, sent_to_all(): return lax.all_to_all(copies, axis, split_axis=0, concat_axis=0, tiled=True)  10.8 us
    dot_general x4, matrix products, gram_of(): jnp.einsum('btd,bsd->bts', cube, cube, preferred_element_type=jnp.float32)  10.8 us
  transfers between devices with their start and end apart: 7, of which 6 were waited for; matrix products, arithmetic and copies ran while one was open for 12% of the time, Pallas kernels for 0%

commit v1 on v0

v1 whole, which is shorter than its diff:
```python
import jax
import jax.numpy as jnp
from jax import lax
from jax.experimental import pallas as pl
from jax.experimental.pallas import tpu as pltpu
from jax.sharding import PartitionSpec as P

inv_root_two = 0.7071067811865476
inv_root_two_pi = 0.3989422804014327

F32, BF16 = jnp.float32, jnp.bfloat16
NX, NY, NZ, NC = 4, 4, 8, 2
IMGS, PATCHES, FEATS = 2, 256, 96
DEPTH, HIDDEN = 1536, 384
HALF = HIDDEN // 2
WIDE = NY * PATCHES
COUNT = NY * IMGS
PEERS = 15
NT = (((1,), (1,)), ((), ()))


def normal_cdf(value):
    return 0.5 * (1.0 + lax.erf(value * inv_root_two))


def mod(value, size):
    return lax.rem(value + size, size)


def kernel(
    x_in, dy_in, w_up, w_down, thresholds,
    grad_up, grad_down, norms_out,
    w_raw, w_rows, full, part, own, relay, got, slope, spread, image_up, image_down,
    sum_up, sum_down, squares, middle, heard, factors, lengths,
    local_sem, first_send, first_self, first_recv, ring_send, ring_recv, twin_send, twin_recv,
    rs_send, rs_recv, ag_send, ag_recv, norm_send, norm_recv, out_sem,
):
    y, m = lax.axis_index("dp"), lax.axis_index("mp")
    c, z, x = lax.rem(m, NC), lax.rem(lax.div(m, NC), NZ), lax.div(m, NC * NZ)

    def device(yy, xx, zz, cc):
        return (yy, (xx * NZ + zz) * NC + cc)

    def plane_peer(k):
        return device(mod(y + k // NX, NY), mod(x + k % NX, NX), z, c)

    def line_peer(k):
        return device(y, x, mod(z + k // NC, NZ), mod(c + k % NC, NC))

    right, left = device(y, x, mod(z + 1, NZ), c), device(y, x, mod(z - 1, NZ), c)
    twin = device(y, x, z, 1 - c)
    above, below = mod(y + 1, NY), mod(y - 1, NY)
    up, down = device(above, x, z, c), device(below, x, z, c)

    def send(src, dst, send_sem, recv_sem, target):
        pltpu.make_async_remote_copy(
            src_ref=src, dst_ref=dst, send_sem=send_sem, recv_sem=recv_sem,
            device_id=target, device_id_type=pl.DeviceIdType.MESH,
        ).start()

    def wait(ref, sem):
        pltpu.make_async_copy(ref, ref, sem).wait()

    up_copy = pltpu.make_async_copy(w_up, w_raw, local_sem.at[0])
    down_copy = pltpu.make_async_copy(w_down, w_rows.at[1], local_sem.at[1])
    up_copy.start()
    down_copy.start()

    barrier = pltpu.get_barrier_semaphore()
    for k in range(1, PEERS + 1):
        for target in (plane_peer(k), line_peer(k)):
            pl.semaphore_signal(
                barrier, inc=1, device_id=target, device_id_type=pl.DeviceIdType.MESH
            )
    pl.semaphore_wait(barrier, 2 * PEERS)

    own_rows = pl.ds(pl.multiple_of((z * NC + c) * FEATS, FEATS), FEATS)
    own_cols = pl.ds(pl.multiple_of(y * PATCHES, PATCHES), PATCHES)
    for t, src in enumerate((x_in, dy_in)):
        for h in range(IMGS):
            dst = full.at[t, h, own_rows, own_cols]
            for k in range(1, NX):
                send(
                    src.at[h], dst, first_send.at[t, h], first_recv.at[t, h],
                    device(x, mod(x + k, NX), z, c),
                )

            @pl.when(x != y)
            def _():
                send(
                    src.at[h], dst, first_self.at[t, h], first_recv.at[t, h], device(x, x, z, c)
                )

            @pl.when(x == y)
            def _():
                pltpu.make_async_copy(src.at[h], dst, first_recv.at[t, h]).start()

    up_copy.wait()
    for k in range(DEPTH // PATCHES):
        span = slice(k * PATCHES, (k + 1) * PATCHES)
        w_rows[0, :, span] = w_raw[span, :].T
    down_copy.wait()

    def chunk(t, h, zz, cols=slice(None)):
        return full.at[t, h, pl.ds(pl.multiple_of((zz * NC + c) * FEATS, FEATS), FEATS), cols]

    def to_twin(t, h, ref):
        send(ref, ref, twin_send.at[t, h], twin_recv.at[t, h], twin)

    def halves(s):
        last = s == NZ // 2 - 1
        return (slice(0, WIDE // 2), slice(WIDE // 2, WIDE)) if last else (slice(None),) * 2

    def ring_step(t, h, s):
        first, second = halves(s)
        ref = chunk(t, h, mod(z - s, NZ), first)
        send(ref, ref, ring_send.at[t, h, 0], ring_recv.at[t, h, 0, s], right)
        ref = chunk(t, h, mod(z + s, NZ), second)
        send(ref, ref, ring_send.at[t, h, 1], ring_recv.at[t, h, 1, s], left)

    def ring_open(t, h):
        mine = full.at[t, h, own_rows, :]
        wait(mine, first_recv.at[t, h])
        ring_step(t, h, 0)
        to_twin(t, h, mine)

    def ring_take(t, h, s):
        first, second = halves(s)
        from_left = chunk(t, h, mod(z - 1 - s, NZ), first)
        from_right = chunk(t, h, mod(z + 1 + s, NZ), second)
        wait(from_left, ring_recv.at[t, h, 0, s])
        wait(from_right, ring_recv.at[t, h, 1, s])
        if s < NZ // 2 - 1:
            ring_step(t, h, s + 1)
        to_twin(t, h, from_left)
        to_twin(t, h, from_right)

    def gathered(t, h):
        wait(full.at[t, h, pl.ds(0, DEPTH // 2), :], twin_recv.at[t, h])

    low, high = slice(0, HALF), slice(HALF, HIDDEN)

    def partials(t, h):
        def body(i, carry):
            shift = jnp.where(i == 0, 2, jnp.where(i == 1, 1, jnp.where(i == 2, 3, 0)))
            owner = lax.rem(y + shift, NY)
            cols = pl.ds(pl.multiple_of(owner * PATCHES, PATCHES), PATCHES)
            value = jnp.dot(w_rows[t], full[t, h, :, cols], preferred_element_type=F32)
            part[t, h, i] = value.astype(BF16)
            own[t, h] = value

            @pl.when(i == 0)
            def _():
                send(
                    part.at[t, h, 0, low, :], relay.at[t, h, 0],
                    rs_send.at[t, h, 0], rs_recv.at[t, h, 0, 0], up,
                )
                send(
                    part.at[t, h, 0, high, :], relay.at[t, h, 1],
                    rs_send.at[t, h, 1], rs_recv.at[t, h, 1, 0], down,
                )

            @pl.when(i == 1)
            def _():
                send(
                    part.at[t, h, 1, high, :], got.at[t, h, 0, high, :],
                    rs_send.at[t, h, 0], rs_recv.at[t, h, 0, 1], up,
                )

            @pl.when(i == 2)
            def _():
                send(
                    part.at[t, h, 2, low, :], got.at[t, h, 1, low, :],
                    rs_send.at[t, h, 1], rs_recv.at[t, h, 1, 1], down,
                )

            return carry

        lax.fori_loop(0, NY, body, 0)

    def relay_partials(t, h):
        for d, (i, rows, target) in enumerate(((1, low, up), (2, high, down))):
            wait(relay.at[t, h, d], rs_recv.at[t, h, d, 0])
            both = part[t, h, i, rows, :].astype(F32) + relay[t, h, d].astype(F32)
            part[t, h, i, rows, :] = both.astype(BF16)
            send(
                part.at[t, h, i, rows, :], got.at[t, h, d, rows, :],
                rs_send.at[t, h, d], rs_recv.at[t, h, d, 2], target,
            )

    def received(t, h):
        wait(got.at[t, h, 0, high, :], rs_recv.at[t, h, 0, 1])
        wait(got.at[t, h, 1, low, :], rs_recv.at[t, h, 1, 1])
        wait(got.at[t, h, 0, low, :], rs_recv.at[t, h, 0, 2])
        wait(got.at[t, h, 1, high, :], rs_recv.at[t, h, 1, 2])

    BAND = 48

    def banded(fn):
        def body(b, carry):
            fn(pl.ds(pl.multiple_of(b * BAND, BAND), BAND))
            return carry

        lax.fori_loop(0, HIDDEN // BAND, body, 0)

    def total(t, h, rows):
        return (
            own[t, h, rows, :]
            + got[t, h, 0, rows, :].astype(F32)
            + got[t, h, 1, rows, :].astype(F32)
        )

    def activate(h):
        def body(rows):
            pre = total(0, h, rows)
            cdf = normal_cdf(pre)
            spread[0, h, y, rows, :] = (pre * cdf).astype(BF16)
            slope[h, rows, :] = cdf + pre * jnp.exp(-0.5 * pre * pre) * inv_root_two_pi

        banded(body)

    def descend(h):
        def body(rows):
            spread[1, h, y, rows, :] = (total(1, h, rows) * slope[h, rows, :]).astype(BF16)

        banded(body)

    def spread_step(t, h, d, j, owner, rows):
        ref = spread.at[t, h, owner, rows, :]
        send(ref, ref, ag_send.at[t, h, d], ag_recv.at[t, h, d, j], (up, down)[d])

    def spread_open(t, h):
        spread_step(t, h, 0, 0, y, low)
        spread_step(t, h, 1, 0, y, high)
        spread_step(t, h, 0, 1, y, high)
        spread_step(t, h, 1, 1, y, low)

    def spread_relay(t, h):
        wait(spread.at[t, h, below, low, :], ag_recv.at[t, h, 0, 0])
        spread_step(t, h, 0, 2, below, low)
        wait(spread.at[t, h, above, high, :], ag_recv.at[t, h, 1, 0])
        spread_step(t, h, 1, 2, above, high)

    def spread_near(t, h):
        wait(spread.at[t, h, below, high, :], ag_recv.at[t, h, 0, 1])
        wait(spread.at[t, h, above, low, :], ag_recv.at[t, h, 1, 1])

    def spread_far(t, h):
        far = mod(y + 2, NY)
        wait(spread.at[t, h, far, low, :], ag_recv.at[t, h, 0, 2])
        wait(spread.at[t, h, far, high, :], ag_recv.at[t, h, 1, 2])

    BLOCK = 512

    def fold(value):
        parts = [value[:, k : k + 128] for k in range(0, value.shape[1], 128)]
        return sum(parts[1:], parts[0])

    def image_of(t, h, owner):
        cols = pl.ds(pl.multiple_of(owner * PATCHES, PATCHES), PATCHES)
        index = owner * IMGS + h

        def body(b, carry):
            span = pl.ds(pl.multiple_of(b * BLOCK, BLOCK), BLOCK)
            if t == 0:
                value = lax.dot_general(
                    full[0, h, span, cols], spread[1, h, owner], NT, preferred_element_type=F32
                )
                image_up[index, span, :] = value.astype(BF16)
            else:
                value = lax.dot_general(
                    spread[0, h, owner], full[1, h, span, cols], NT, preferred_element_type=F32
                )
                image_down[index, :, span] = value.astype(BF16)
            return carry + fold(jnp.sum(value * value, axis=0, keepdims=True))

        start = jnp.zeros((1, 128), F32)
        squares[t, pl.ds(index, 1), :] = lax.fori_loop(0, DEPTH // BLOCK, body, start)

    def all_images(t, h):
        def body(i, carry):
            image_of(t, h, lax.rem(y + i, NY))
            return carry

        lax.fori_loop(0, NY, body, 0)

    def images_as_they_come(h):
        def body(i, carry):
            @pl.when(i == 1)
            def _():
                spread_relay(1, h)
                spread_near(1, h)

            @pl.when(i == 3)
            def _():
                spread_far(1, h)

            shift = jnp.where(i == 0, 0, jnp.where(i == 1, 1, jnp.where(i == 2, 3, 2)))
            image_of(0, h, lax.rem(y + shift, NY))
            return carry

        lax.fori_loop(0, NY, body, 0)

    def norm_open(t):
        for k in range(1, PEERS + 1):
            send(
                squares.at[t], heard.at[t, 0, k - 1],
                norm_send.at[t, 0], norm_recv.at[t, 0], plane_peer(k),
            )

    def norm_middle(t):
        wait(heard.at[t, 0], norm_recv.at[t, 0])
        middle[t] = squares[t] + jnp.sum(heard[t, 0], axis=0)
        for k in range(1, PEERS + 1):
            send(
                middle.at[t], heard.at[t, 1, k - 1],
                norm_send.at[t, 1], norm_recv.at[t, 1], line_peer(k),
            )

    def norm_close(t):
        wait(heard.at[t, 1], norm_recv.at[t, 1])
        lanes = middle[t] + jnp.sum(heard[t, 1], axis=0)
        length = jnp.sqrt(jnp.sum(lanes, axis=1, keepdims=True))
        factor = jnp.minimum(1.0, thresholds[t] / (length + 1e-06))
        lengths[t] = jnp.broadcast_to(length, (COUNT, 128))
        factors[t] = jnp.broadcast_to(factor, (COUNT, 128))

    def combine(t, images, sums, out, rows_each, pieces):
        size = sums.shape[0] // pieces
        for p in range(pieces):

            def body(b, carry):
                start = p * size + b * rows_each
                rows = pl.ds(pl.multiple_of(start, rows_each), rows_each)
                for k in range(0, sums.shape[1], 384):
                    cols = slice(k, k + 384)
                    acc = None
                    for i in range(COUNT):
                        factor = jnp.tile(factors[t, i : i + 1, :], (1, 3))
                        term = images[i, rows, cols].astype(F32) * factor
                        acc = term if acc is None else acc + term
                    sums[rows, cols] = acc
                return carry

            lax.fori_loop(0, size // rows_each, body, 0)
            rows = slice(p * size, (p + 1) * size)
            pltpu.make_async_copy(sums.at[rows, :], out.at[rows, :], out_sem.at[t, p]).start()

    def combine_wait(t, sums, out, pieces):
        size = sums.shape[0] // pieces
        for p in range(pieces):
            rows = slice(p * size, (p + 1) * size)
            pltpu.make_async_copy(sums.at[rows, :], out.at[rows, :], out_sem.at[t, p]).wait()

    steps = NZ // 2
    for h in range(IMGS):
        ring_open(0, h)
    for s in range(steps - 1):
        for h in range(IMGS):
            ring_take(0, h, s)
    for h in range(IMGS):
        ring_open(1, h)
    for h in range(IMGS):
        ring_take(0, h, steps - 1)
    for h in range(IMGS):
        gathered(0, h)
        partials(0, h)
    relay_partials(0, 0)
    relay_partials(0, 1)
    for h in range(IMGS):
        ring_take(1, h, 0)
    for h in range(IMGS):
        received(0, h)
        activate(h)
        spread_open(0, h)
    for h in range(IMGS):
        ring_take(1, h, 1)
    for h in range(IMGS):
        spread_relay(0, h)
    for h in range(IMGS):
        ring_take(1, h, 2)
    for h in range(IMGS):
        ring_take(1, h, 3)
    for h in range(IMGS):
        spread_near(0, h)
        spread_far(0, h)
    for h in range(IMGS):
        gathered(1, h)
        partials(1, h)
    relay_partials(1, 0)
    all_images(1, 0)
    relay_partials(1, 1)
    received(1, 0)
    descend(0)
    spread_open(1, 0)
    all_images(1, 1)
    received(1, 1)
    descend(1)
    spread_open(1, 1)
    norm_open(1)
    images_as_they_come(0)
    norm_middle(1)
    images_as_they_come(1)
    norm_open(0)
    norm_close(1)
    combine(1, image_down, sum_down, grad_down, 16, 2)
    norm_middle(0)
    norm_close(0)
    combine(0, image_up, sum_up, grad_up, 16, 4)

    mine = pl.ds(y * IMGS, IMGS)
    lane = lax.broadcasted_iota(jnp.int32, (IMGS, 128), 1)
    both = jnp.where(lane == 0, lengths[0, mine, :], lengths[1, mine, :])
    norms_out[...] = both[:, :2]

    for t in range(2):
        for h in range(IMGS):
            wait(full.at[t, h, pl.ds(0, FEATS), pl.ds(0, 3 * PATCHES)], first_send.at[t, h])

            @pl.when(x != y)
            def _():
                wait(full.at[t, h, pl.ds(0, FEATS), pl.ds(0, PATCHES)], first_self.at[t, h])

            wait(full.at[t, h, pl.ds(0, DEPTH // 2), :], twin_send.at[t, h])
            for d in range(2):
                wait(full.at[t, h, pl.ds(0, FEATS * 7 // 2), :], ring_send.at[t, h, d])
                three = full.at[t, h, pl.ds(0, 3 * HALF), pl.ds(0, PATCHES)]
                wait(three, rs_send.at[t, h, d])
                wait(three, ag_send.at[t, h, d])
        for stage in range(2):
            wait(heard.at[t, stage], norm_send.at[t, stage])
    combine_wait(1, sum_down, grad_down, 2)
    combine_wait(0, sum_up, grad_up, 4)


def on_device(inputs, cotangent, w_up, w_down, thresholds):
    x_t = jnp.swapaxes(inputs, 1, 2)
    dy_t = jnp.swapaxes(cotangent, 1, 2)
    vmem, hbm = pl.BlockSpec(memory_space=pltpu.VMEM), pl.BlockSpec(memory_space=pl.ANY)
    dma = pltpu.SemaphoreType.DMA
    return pl.pallas_call(
        kernel,
        out_shape=(
            jax.ShapeDtypeStruct((DEPTH, HIDDEN), F32),
            jax.ShapeDtypeStruct((HIDDEN, DEPTH), F32),
            jax.ShapeDtypeStruct((IMGS, 2), F32),
        ),
        in_specs=[vmem, vmem, hbm, hbm, pl.BlockSpec(memory_space=pltpu.SMEM)],
        out_specs=(hbm, hbm, vmem),
        scratch_shapes=[
            pltpu.VMEM((DEPTH, HIDDEN), BF16),
            pltpu.VMEM((2, HIDDEN, DEPTH), BF16),
            pltpu.VMEM((2, IMGS, DEPTH, WIDE), BF16),
            pltpu.VMEM((2, IMGS, NY, HIDDEN, PATCHES), BF16),
            pltpu.VMEM((2, IMGS, HIDDEN, PATCHES), F32),
            pltpu.VMEM((2, IMGS, 2, HALF, PATCHES), BF16),
            pltpu.VMEM((2, IMGS, 2, HIDDEN, PATCHES), BF16),
            pltpu.VMEM((IMGS, HIDDEN, PATCHES), F32),
            pltpu.VMEM((2, IMGS, NY, HIDDEN, PATCHES), BF16),
            pltpu.VMEM((COUNT, DEPTH, HIDDEN), BF16),
            pltpu.VMEM((COUNT, HIDDEN, DEPTH), BF16),
            pltpu.VMEM((DEPTH, HIDDEN), F32),
            pltpu.VMEM((HIDDEN, DEPTH), F32),
            pltpu.VMEM((2, COUNT, 128), F32),
            pltpu.VMEM((2, COUNT, 128), F32),
            pltpu.VMEM((2, 2, PEERS, COUNT, 128), F32),
            pltpu.VMEM((2, COUNT, 128), F32),
            pltpu.VMEM((2, COUNT, 128), F32),
            dma((2,)),
            dma((2, IMGS)),
            dma((2, IMGS)),
            dma((2, IMGS)),
            dma((2, IMGS, 2)),
            dma((2, IMGS, 2, NZ // 2)),
            dma((2, IMGS)),
            dma((2, IMGS)),
            dma((2, IMGS, 2)),
            dma((2, IMGS, 2, 3)),
            dma((2, IMGS, 2)),
            dma((2, IMGS, 2, 3)),
            dma((2, 2)),
            dma((2, 2)),
            dma((2, 4)),
        ],
        compiler_params=pltpu.CompilerParams(
            collective_id=0, has_side_effects=True, vmem_limit_bytes=66 * 2**20 - 2**21
        ),
        name="clipped_backward",
    )(x_t, dy_t, w_up, w_down, thresholds)


def solution(mesh):
    in_specs = (P("dp", None, "mp"), P("dp", None, "mp"), P("dp", "mp"), P("mp", "dp"), P())
    out_specs = (P("dp", "mp"), P("mp", "dp"), P("dp", None))
    return jax.shard_map(
        on_device, mesh=mesh, in_specs=in_specs, out_specs=out_specs, check_vma=False
    )
```

time: 446 us -> 138 us (0.31)
  waiting for transfers between devices: 330 us -> 0 us
  Pallas kernels: 0 us -> 132 us
  matrix products: 39.5 us -> 0 us
  local copies, waits for them, and re-layouts: 32.9 us -> 5.35 us
  starting transfers between devices: 16.1 us -> 0 us
  between operations: 13.9 us -> 0.65 us
  other arithmetic: 12.4 us -> 0 us
    all_gather x4 -> x0, waiting for transfers between devices: 252 us -> none  [the longest x1 85.6 us: on_device(): lax.all_gather(inputs, 'mp', axis=2, tiled=True).reshape(count_rows, -1)]
    pallas_call x0 -> x1, Pallas kernels: none -> 132 us  [on_device(): pl.pallas_call(kernel, out_shape=(jax.ShapeDtypeStruct((DEPTH, HIDDEN), F...]
    all_to_all x2 -> x0, waiting for transfers between devices: 76.1 us -> none  [the longest x1 67.2 us: sum_at_owner(): lax.all_to_all(pieces, axis, split_axis=0, concat_axis=0, tiled=True)]
    dot_general x8 -> x0, matrix products: 39.5 us -> none  [the longest x4 10.8 us: gram_of(): jnp.einsum('btd,bsd->bts', cube, cube, preferred_element_type=jnp.float32)]
    all_gather x2 -> x0, local copies, waits for them, and re-layouts: 17.4 us -> none  [the longest x1 8.68 us: on_device(): lax.all_gather(cotangent, 'mp', axis=2, tiled=True).reshape(count_rows, -1)]
    all_to_all x2 -> x0, starting transfers between devices: 15.8 us -> none  [the longest x1 10.8 us: sent_to_all(): return lax.all_to_all(copies, axis, split_axis=0, concat_axis=0, tiled=True)]
    convert_element_type x1 -> x0, local copies, waits for them, and re-layouts: 8.68 us -> none  [on_device(): cot_clip = (factor[:, 1][:, None, None] * dy_whole.reshape(images, patche...]
    convert_element_type x1 -> x0, other arithmetic: 7.52 us -> none  [on_device(): cot_clip = (factor[:, 1][:, None, None] * dy_whole.reshape(images, patche...]
  transfers between devices with their start and end apart: 7 -> 0, of which waited for: 6 -> 0; matrix products, arithmetic and copies ran while one was open for 12% -> 0% of each run, Pallas kernels for 0% -> 0%
where the time goes in v1:
time: 138 us
  Pallas kernels  132 us (96%)
  local copies, waits for them, and re-layouts  5.35 us (4%)
    pallas_call x1, Pallas kernels, on_device(): pl.pallas_call(kernel, out_shape=(jax.ShapeDtypeStruct((DEPTH, HIDDEN), F...  132 us
    unnamed x7, local copies, waits for them, and re-layouts  5.35 us

profile of v1, /device:TPU:1, one launch (start us, length us, event | category | flops | bytes accessed | tf_op | source)
XLA Modules:
  0.0 137.9 jit_solution(13641641441620885884)
XLA Ops:
  0.6 131.9 %clipped_backward.1 = (f32[1536,384]{1,0:T(8,128)}, f32[384,1536]{1,0:T(8,128)}, f32[2,2]{1,0:T(2,128)}) custom-call(bf16[2,96,256]{2,1,0:T(8,128)(2,1)} %bitcast.2, bf16[2,96,256]{2,1,0:T(8,128)(2,1)} %bitcast.3, bf16[1536,384]{1,0:T(8,128)(2,1)} %w_up.1, bf16[384,1536]{1,0:T(8,128)(2,1)} %w_down.1, f32[2]{0:T(128)} %thresholds.1), custom_call_target="tpu_custom_call" | custom-call | tf_op jit(solution)/shard_map/clipped_backward/pallas_call | solution.py:441
  132.5 0.0 copy-start
  132.6 3.4 %copy.11 = f32[1536,384]{1,0:T(8,128)} copy(f32[1536,384]{1,0:T(8,128)} %get-tuple-element.6) | data formatting | bytes 4718592
  135.9 0.0 copy-done
  135.9 0.0 copy-start.1
  135.9 1.4 %copy.12 = f32[384,1536]{1,0:T(8,128)} copy(f32[384,1536]{1,0:T(8,128)S(1)} %copy-done) | data formatting | bytes 4718592
  137.3 0.0 copy-done.1
  137.3 0.6 copy.13
Async XLA Ops:
  132.5 3.4 %copy-start = (f32[384,1536]{1,0:T(8,128)S(1)}, f32[384,1536]{1,0:T(8,128)}, u32[]{:S(2)}) copy-start(f32[384,1536]{1,0:T(8,128)} %get-tuple-element.7) | copy-start | bytes 7077892
  135.9 1.4 %copy-start.1 = (f32[2,2]{1,0:T(2,128)S(1)}, f32[2,2]{1,0:T(2,128)}, u32[]{:S(2)}) copy-start(f32[2,2]{1,0:T(2,128)} %get-tuple-element.8) | copy-start | bytes 52
